TPU v7x, 512 devices: a whole 4x4x16 slice. The times are simulated.
512 devices in a mesh: ctx: 32 (over z, core), ch: 16 (over x, y).
Axes of the slice: x: 4, y: 4, z: 16, core: 2. Of those that a mesh axis runs over, the one named last changes fastest.
Arguments:
- signal: bfloat16 [4096, 8192], P('ctx', 'ch'), may hold values from -170 to 170, as said below
- norm_gain: float32 [8192], P('ch'), may hold values from 0.1 to 1.9
- skip_gain: float32 [8192], P('ch'), may hold values from 0.5 to 1.5
- filter_taps: bfloat16 [4096, 8192], P('ctx', 'ch'), may hold values from -1.5 to 1.5, as said below
- out_gate: bfloat16 [4096, 8192], P('ctx', 'ch'), may hold values from -6 to 6
Outputs:
- mixture: bfloat16 [4096, 8192], P('ctx', 'ch')
Inputs may be any that keep to these rules, and one draw needn't show every extreme that they name: `signal`: features whose channels and tokens have different scales. `filter_taps`: a filter whose taps fall off along the lags at a rate that differs between channels.
All inputs are finite; a program needn't handle non-finite values.
Results may differ from a plain program's by a relative error of at most 0.006.
Values may be sent and summed in bfloat16 or wider, within the bound.
A program may use at most 64 MiB of HBM per device.

v0:
```python
import math
import jax
import jax.numpy as jnp
from jax import lax
from jax.sharding import PartitionSpec as P

C = 8192
EPS = 1e-06


def passed_along(block, axis, distance):
    devices = range(lax.axis_size(axis))
    route = [(i - distance, i) for i in devices if i - distance in devices]
    return lax.ppermute(block, axis, route)


def split_parts(matrix):
    high = matrix.astype(jnp.bfloat16)
    kept = lax.optimization_barrier(high)
    low = (matrix - kept.astype(jnp.float32)).astype(jnp.bfloat16)
    return (high, low)


def table_dot(table_pair, data):
    return jnp.dot(table_pair[0], data, preferred_element_type=jnp.float32) + jnp.dot(
        table_pair[1], data, preferred_element_type=jnp.float32
    )


def fine_dot(table_pair, data):
    data_high, data_low = split_parts(data)
    return (
        jnp.dot(table_pair[0], data_high, preferred_element_type=jnp.float32)
        + jnp.dot(table_pair[0], data_low, preferred_element_type=jnp.float32)
        + jnp.dot(table_pair[1], data_high, preferred_element_type=jnp.float32)
    )


def dft_tables(tok_rows):
    freq_ids = jnp.arange(tok_rows + 1, dtype=jnp.int32)
    row_ids = jnp.arange(tok_rows, dtype=jnp.int32)
    out_ids = jnp.arange(2 * tok_rows, dtype=jnp.int32)
    fwd_phase = (freq_ids[:, None] * row_ids[None, :] % (2 * tok_rows)).astype(jnp.float32) * (
        math.pi / tok_rows
    )
    inv_phase = (out_ids[:, None] * freq_ids[None, :] % (2 * tok_rows)).astype(jnp.float32) * (
        math.pi / tok_rows
    )
    weights = jnp.where((freq_ids == 0) | (freq_ids == tok_rows), 1.0, 2.0).astype(jnp.float32) / (
        2.0 * tok_rows
    )
    return (
        jnp.cos(fwd_phase),
        jnp.sin(fwd_phase),
        jnp.cos(inv_phase) * weights[None, :],
        jnp.sin(inv_phase) * weights[None, :],
    )


def local(signal, norm_gain, skip_gain, filter_taps, out_gate):
    tok_rows, channels = signal.shape
    ctx_count = lax.axis_size("ctx")
    ctx_index = lax.axis_index("ctx")
    values = signal.astype(jnp.float32)
    row_power = lax.psum(jnp.sum(values * values, axis=1), "ch") / C
    normed = (values * lax.rsqrt(row_power + EPS)[:, None] * norm_gain[None, :]).astype(
        jnp.bfloat16
    )
    fwd_cos, fwd_sin, inv_cos, inv_sin = dft_tables(tok_rows)
    cos_high, cos_low = split_parts(fwd_cos)
    sin_high, sin_low = split_parts(fwd_sin)
    halfway = ctx_count // 2
    quarter = ctx_count // 4
    helper = jnp.zeros((), jnp.bool_)
    first_own = jnp.zeros((), jnp.int32)
    partner = ctx_index + halfway
    whole_filter = lax.all_gather(filter_taps, "ctx", axis=0, tiled=True)

    def spectrum(segment):
        span_rows = segment.shape[0]
        cos_pair = (cos_high, cos_low)
        sin_pair = (sin_high, sin_low)
        return (table_dot(cos_pair, segment), -table_dot(sin_pair, segment))

    def lag_product(lag_block, sig_re, sig_im, sum_re, sum_im):
        taps = lax.dynamic_slice_in_dim(whole_filter, lag_block * tok_rows, tok_rows, 0)
        fil_re, fil_im = spectrum(taps)
        return (
            sum_re + fil_re * sig_re - fil_im * sig_im,
            sum_im + fil_re * sig_im + fil_im * sig_re,
        )

    blank = jnp.zeros((tok_rows + 1, channels), jnp.float32)
    segment_in = lax.all_gather(normed, "ctx", axis=0, tiled=True)
    span_rows = min(segment_in.shape[0], tok_rows)

    def one_span(sub_index, running):
        anchor = sub_index * span_rows
        segment = lax.dynamic_slice_in_dim(segment_in, sub_index * span_rows, span_rows, 0)
        source = anchor // tok_rows
        own_ok = (source <= ctx_index) & (source >= first_own)
        help_ok = helper & (source < quarter)

        def do_work(state):
            sig_re, sig_im = spectrum(segment)

            def own_add(pair_in):
                return lag_product(ctx_index - source, sig_re, sig_im, pair_in[0], pair_in[1])

            def help_add(pair_in):
                return lag_product(partner - source, sig_re, sig_im, pair_in[0], pair_in[1])

            def keep_pair(pair_in):
                return pair_in

            own_re, own_im = lax.cond(own_ok, own_add, keep_pair, (state[0], state[1]))
            help_re, help_im = lax.cond(help_ok, help_add, keep_pair, (state[2], state[3]))
            return (own_re, own_im, help_re, help_im)

        def skip_work(state):
            return state

        return lax.cond(own_ok | help_ok, do_work, skip_work, running)

    own_re, own_im, help_re, help_im = lax.fori_loop(
        0, segment_in.shape[0] // span_rows, one_span, (blank, blank, blank, blank)
    )
    low_cos = split_parts(inv_cos[:tok_rows])
    low_sin = split_parts(inv_sin[:tok_rows])
    high_cos = split_parts(inv_cos[tok_rows:])
    high_sin = split_parts(inv_sin[tok_rows:])
    low_part = fine_dot(low_cos, own_re) - fine_dot(low_sin, own_im)
    high_part = fine_dot(high_cos, own_re) - fine_dot(high_sin, own_im)
    convolved = low_part + passed_along(high_part.astype(jnp.bfloat16), "ctx", 1).astype(
        high_part.dtype
    )
    mixture = out_gate.astype(jnp.float32) * (
        convolved + skip_gain[None, :] * normed.astype(jnp.float32)
    )
    return mixture.astype(jnp.bfloat16)


def solution(mesh):
    return jax.shard_map(
        local,
        mesh=mesh,
        in_specs=(P("ctx", "ch"), P("ch"), P("ch"), P("ctx", "ch"), P("ctx", "ch")),
        out_specs=P("ctx", "ch"),
        check_vma=False,
    )
```

profile of v0, /device:TPU:483, one launch (start us, length us, event | category | flops | bytes accessed | tf_op | source)
XLA Modules:
  0.0 462.2 jit_solution(6223332939443053521)
XLA Ops:
  8.3 28.1 %psum.7 = f32[128]{0:T(128)S(1)} all-reduce(f32[128]{0:T(128)S(1)} %fusion.33), channel_id=1, replica_groups=mesh['ctx'=32,'ch'=16] {'ch'}, use_global_device_ids=true, to_apply=%region_1.0 | all-reduce | flops 128 | bytes 1024 | tf_op jit(solution)/shard_map/psum | solution.py:65
  40.1 41.6 %all-gather.5.cloned.1.call-done = bf16[4096,512]{1,0:T(8,128)(2,1)} async-done(((bf16[128,512]{1,0:T(8,128)(2,1)}), bf16[4096,512]{1,0:T(8,128)(2,1)}) %all-gather.5.cloned.1.call-update) | async-done | bytes 4194320 | tf_op jit(solution)/shard_map/all_gather | solution.py:77
  81.7 72.9 %all-gather.3.cloned.1.call-done = bf16[4096,512]{1,0:T(8,128)(2,1)} async-done(((bf16[128,512]{1,0:T(8,128)(2,1)}), bf16[4096,512]{1,0:T(8,128)(2,1)}) %all-gather.3.cloned.1.call-update) | async-done | bytes 4194320 | tf_op jit(solution)/shard_map/all_gather | solution.py:94
  154.6 294.8 %while.19 = (s32[]{:T(128)}, f32[129,512]{1,0:T(8,128)S(1)}, f32[129,512]{1,0:T(8,128)S(1)}, s32[]{:T(128)}, bf16[4096,512]{1,0:T(8,128)(2,1)}, /*index=5*/bf16[...) while((s32[]{:T(128)}, f32[129,512]{1,0:T(8,128)S(1)}, ...), condition=%wide.region_7.8_spmd.clone.clone, body=%wide.region_2.7_spmd.clone.clone.sunk | while | flops 136455184 | bytes 6134993 | solution.py:125
  155.0 8.9 %conditional.5 = ((f32[129,512]{1,0:T(8,128)S(1)}, f32[129,512]{1,0:T(8,128)S(1)})) conditional(s32[]{:T(128)} %convert_element_type.331, (f32[129,512]{1,0:T(8,128)S(1)}, f32[129,512]{1,0:T(8,128)S(1)}) %tuple.76, (pred[]{:T(512)}, s32[]{:T(128)}, pred[]{:T(512)}, bf16[4096,512]{1,0:T(8,128)(2,1)}, bf16[129,128]{1,0:T(8,128)(2,1)S(1)}, ...), branch_computations={%region_3.3_spmd, %region_4.6_spmd} | conditional | flops 136190976 | bytes 6068488 | solution.py:123
  159.4 4.5 conditional
  164.2 8.9 %conditional.5 = ((f32[129,512]{1,0:T(8,128)S(1)}, f32[129,512]{1,0:T(8,128)S(1)})) conditional(s32[]{:T(128)} %convert_element_type.331, (f32[129,512]{1,0:T(8,128)S(1)}, f32[129,512]{1,0:T(8,128)S(1)}) %tuple.76, (pred[]{:T(512)}, s32[]{:T(128)}, pred[]{:T(512)}, bf16[4096,512]{1,0:T(8,128)(2,1)}, bf16[129,128]{1,0:T(8,128)(2,1)S(1)}, ...), branch_computations={%region_3.3_spmd, %region_4.6_spmd} | conditional | flops 136190976 | bytes 6068488 | solution.py:123
  168.6 4.5 conditional
  173.4 8.9 %conditional.5 = ((f32[129,512]{1,0:T(8,128)S(1)}, f32[129,512]{1,0:T(8,128)S(1)})) conditional(s32[]{:T(128)} %convert_element_type.331, (f32[129,512]{1,0:T(8,128)S(1)}, f32[129,512]{1,0:T(8,128)S(1)}) %tuple.76, (pred[]{:T(512)}, s32[]{:T(128)}, pred[]{:T(512)}, bf16[4096,512]{1,0:T(8,128)(2,1)}, bf16[129,128]{1,0:T(8,128)(2,1)S(1)}, ...), branch_computations={%region_3.3_spmd, %region_4.6_spmd} | conditional | flops 136190976 | bytes 6068488 | solution.py:123
  177.8 4.5 conditional
  182.6 8.9 %conditional.5 = ((f32[129,512]{1,0:T(8,128)S(1)}, f32[129,512]{1,0:T(8,128)S(1)})) conditional(s32[]{:T(128)} %convert_element_type.331, (f32[129,512]{1,0:T(8,128)S(1)}, f32[129,512]{1,0:T(8,128)S(1)}) %tuple.76, (pred[]{:T(512)}, s32[]{:T(128)}, pred[]{:T(512)}, bf16[4096,512]{1,0:T(8,128)(2,1)}, bf16[129,128]{1,0:T(8,128)(2,1)S(1)}, ...), branch_computations={%region_3.3_spmd, %region_4.6_spmd} | conditional | flops 136190976 | bytes 6068488 | solution.py:123
  187.0 4.5 conditional
  191.8 8.9 %conditional.5 = ((f32[129,512]{1,0:T(8,128)S(1)}, f32[129,512]{1,0:T(8,128)S(1)})) conditional(s32[]{:T(128)} %convert_element_type.331, (f32[129,512]{1,0:T(8,128)S(1)}, f32[129,512]{1,0:T(8,128)S(1)}) %tuple.76, (pred[]{:T(512)}, s32[]{:T(128)}, pred[]{:T(512)}, bf16[4096,512]{1,0:T(8,128)(2,1)}, bf16[129,128]{1,0:T(8,128)(2,1)S(1)}, ...), branch_computations={%region_3.3_spmd, %region_4.6_spmd} | conditional | flops 136190976 | bytes 6068488 | solution.py:123
  196.2 4.5 conditional
  201.0 8.9 %conditional.5 = ((f32[129,512]{1,0:T(8,128)S(1)}, f32[129,512]{1,0:T(8,128)S(1)})) conditional(s32[]{:T(128)} %convert_element_type.331, (f32[129,512]{1,0:T(8,128)S(1)}, f32[129,512]{1,0:T(8,128)S(1)}) %tuple.76, (pred[]{:T(512)}, s32[]{:T(128)}, pred[]{:T(512)}, bf16[4096,512]{1,0:T(8,128)(2,1)}, bf16[129,128]{1,0:T(8,128)(2,1)S(1)}, ...), branch_computations={%region_3.3_spmd, %region_4.6_spmd} | conditional | flops 136190976 | bytes 6068488 | solution.py:123
  205.4 4.5 conditional
  210.3 8.9 %conditional.5 = ((f32[129,512]{1,0:T(8,128)S(1)}, f32[129,512]{1,0:T(8,128)S(1)})) conditional(s32[]{:T(128)} %convert_element_type.331, (f32[129,512]{1,0:T(8,128)S(1)}, f32[129,512]{1,0:T(8,128)S(1)}) %tuple.76, (pred[]{:T(512)}, s32[]{:T(128)}, pred[]{:T(512)}, bf16[4096,512]{1,0:T(8,128)(2,1)}, bf16[129,128]{1,0:T(8,128)(2,1)S(1)}, ...), branch_computations={%region_3.3_spmd, %region_4.6_spmd} | conditional | flops 136190976 | bytes 6068488 | solution.py:123
  214.6 4.5 conditional
  219.5 8.9 %conditional.5 = ((f32[129,512]{1,0:T(8,128)S(1)}, f32[129,512]{1,0:T(8,128)S(1)})) conditional(s32[]{:T(128)} %convert_element_type.331, (f32[129,512]{1,0:T(8,128)S(1)}, f32[129,512]{1,0:T(8,128)S(1)}) %tuple.76, (pred[]{:T(512)}, s32[]{:T(128)}, pred[]{:T(512)}, bf16[4096,512]{1,0:T(8,128)(2,1)}, bf16[129,128]{1,0:T(8,128)(2,1)S(1)}, ...), branch_computations={%region_3.3_spmd, %region_4.6_spmd} | conditional | flops 136190976 | bytes 6068488 | solution.py:123
  223.8 4.5 conditional
  228.7 8.9 %conditional.5 = ((f32[129,512]{1,0:T(8,128)S(1)}, f32[129,512]{1,0:T(8,128)S(1)})) conditional(s32[]{:T(128)} %convert_element_type.331, (f32[129,512]{1,0:T(8,128)S(1)}, f32[129,512]{1,0:T(8,128)S(1)}) %tuple.76, (pred[]{:T(512)}, s32[]{:T(128)}, pred[]{:T(512)}, bf16[4096,512]{1,0:T(8,128)(2,1)}, bf16[129,128]{1,0:T(8,128)(2,1)S(1)}, ...), branch_computations={%region_3.3_spmd, %region_4.6_spmd} | conditional | flops 136190976 | bytes 6068488 | solution.py:123
  233.1 4.5 conditional
  237.9 8.9 %conditional.5 = ((f32[129,512]{1,0:T(8,128)S(1)}, f32[129,512]{1,0:T(8,128)S(1)})) conditional(s32[]{:T(128)} %convert_element_type.331, (f32[129,512]{1,0:T(8,128)S(1)}, f32[129,512]{1,0:T(8,128)S(1)}) %tuple.76, (pred[]{:T(512)}, s32[]{:T(128)}, pred[]{:T(512)}, bf16[4096,512]{1,0:T(8,128)(2,1)}, bf16[129,128]{1,0:T(8,128)(2,1)S(1)}, ...), branch_computations={%region_3.3_spmd, %region_4.6_spmd} | conditional | flops 136190976 | bytes 6068488 | solution.py:123
  242.3 4.5 conditional
  247.1 8.9 %conditional.5 = ((f32[129,512]{1,0:T(8,128)S(1)}, f32[129,512]{1,0:T(8,128)S(1)})) conditional(s32[]{:T(128)} %convert_element_type.331, (f32[129,512]{1,0:T(8,128)S(1)}, f32[129,512]{1,0:T(8,128)S(1)}) %tuple.76, (pred[]{:T(512)}, s32[]{:T(128)}, pred[]{:T(512)}, bf16[4096,512]{1,0:T(8,128)(2,1)}, bf16[129,128]{1,0:T(8,128)(2,1)S(1)}, ...), branch_computations={%region_3.3_spmd, %region_4.6_spmd} | conditional | flops 136190976 | bytes 6068488 | solution.py:123
  251.5 4.5 conditional
  256.3 8.9 %conditional.5 = ((f32[129,512]{1,0:T(8,128)S(1)}, f32[129,512]{1,0:T(8,128)S(1)})) conditional(s32[]{:T(128)} %convert_element_type.331, (f32[129,512]{1,0:T(8,128)S(1)}, f32[129,512]{1,0:T(8,128)S(1)}) %tuple.76, (pred[]{:T(512)}, s32[]{:T(128)}, pred[]{:T(512)}, bf16[4096,512]{1,0:T(8,128)(2,1)}, bf16[129,128]{1,0:T(8,128)(2,1)S(1)}, ...), branch_computations={%region_3.3_spmd, %region_4.6_spmd} | conditional | flops 136190976 | bytes 6068488 | solution.py:123
  260.7 4.5 conditional
  265.5 8.9 %conditional.5 = ((f32[129,512]{1,0:T(8,128)S(1)}, f32[129,512]{1,0:T(8,128)S(1)})) conditional(s32[]{:T(128)} %convert_element_type.331, (f32[129,512]{1,0:T(8,128)S(1)}, f32[129,512]{1,0:T(8,128)S(1)}) %tuple.76, (pred[]{:T(512)}, s32[]{:T(128)}, pred[]{:T(512)}, bf16[4096,512]{1,0:T(8,128)(2,1)}, bf16[129,128]{1,0:T(8,128)(2,1)S(1)}, ...), branch_computations={%region_3.3_spmd, %region_4.6_spmd} | conditional | flops 136190976 | bytes 6068488 | solution.py:123
  269.9 4.5 conditional
  274.7 8.9 %conditional.5 = ((f32[129,512]{1,0:T(8,128)S(1)}, f32[129,512]{1,0:T(8,128)S(1)})) conditional(s32[]{:T(128)} %convert_element_type.331, (f32[129,512]{1,0:T(8,128)S(1)}, f32[129,512]{1,0:T(8,128)S(1)}) %tuple.76, (pred[]{:T(512)}, s32[]{:T(128)}, pred[]{:T(512)}, bf16[4096,512]{1,0:T(8,128)(2,1)}, bf16[129,128]{1,0:T(8,128)(2,1)S(1)}, ...), branch_computations={%region_3.3_spmd, %region_4.6_spmd} | conditional | flops 136190976 | bytes 6068488 | solution.py:123
  279.1 4.5 conditional
  284.0 8.9 %conditional.5 = ((f32[129,512]{1,0:T(8,128)S(1)}, f32[129,512]{1,0:T(8,128)S(1)})) conditional(s32[]{:T(128)} %convert_element_type.331, (f32[129,512]{1,0:T(8,128)S(1)}, f32[129,512]{1,0:T(8,128)S(1)}) %tuple.76, (pred[]{:T(512)}, s32[]{:T(128)}, pred[]{:T(512)}, bf16[4096,512]{1,0:T(8,128)(2,1)}, bf16[129,128]{1,0:T(8,128)(2,1)S(1)}, ...), branch_computations={%region_3.3_spmd, %region_4.6_spmd} | conditional | flops 136190976 | bytes 6068488 | solution.py:123
  288.3 4.5 conditional
  293.2 8.9 %conditional.5 = ((f32[129,512]{1,0:T(8,128)S(1)}, f32[129,512]{1,0:T(8,128)S(1)})) conditional(s32[]{:T(128)} %convert_element_type.331, (f32[129,512]{1,0:T(8,128)S(1)}, f32[129,512]{1,0:T(8,128)S(1)}) %tuple.76, (pred[]{:T(512)}, s32[]{:T(128)}, pred[]{:T(512)}, bf16[4096,512]{1,0:T(8,128)(2,1)}, bf16[129,128]{1,0:T(8,128)(2,1)S(1)}, ...), branch_computations={%region_3.3_spmd, %region_4.6_spmd} | conditional | flops 136190976 | bytes 6068488 | solution.py:123
  297.5 4.5 conditional
  302.4 8.9 %conditional.5 = ((f32[129,512]{1,0:T(8,128)S(1)}, f32[129,512]{1,0:T(8,128)S(1)})) conditional(s32[]{:T(128)} %convert_element_type.331, (f32[129,512]{1,0:T(8,128)S(1)}, f32[129,512]{1,0:T(8,128)S(1)}) %tuple.76, (pred[]{:T(512)}, s32[]{:T(128)}, pred[]{:T(512)}, bf16[4096,512]{1,0:T(8,128)(2,1)}, bf16[129,128]{1,0:T(8,128)(2,1)S(1)}, ...), branch_computations={%region_3.3_spmd, %region_4.6_spmd} | conditional | flops 136190976 | bytes 6068488 | solution.py:123
  306.8 4.5 conditional
  311.6 8.9 %conditional.5 = ((f32[129,512]{1,0:T(8,128)S(1)}, f32[129,512]{1,0:T(8,128)S(1)})) conditional(s32[]{:T(128)} %convert_element_type.331, (f32[129,512]{1,0:T(8,128)S(1)}, f32[129,512]{1,0:T(8,128)S(1)}) %tuple.76, (pred[]{:T(512)}, s32[]{:T(128)}, pred[]{:T(512)}, bf16[4096,512]{1,0:T(8,128)(2,1)}, bf16[129,128]{1,0:T(8,128)(2,1)S(1)}, ...), branch_computations={%region_3.3_spmd, %region_4.6_spmd} | conditional | flops 136190976 | bytes 6068488 | solution.py:123
  316.0 4.5 conditional
  320.8 8.9 %conditional.5 = ((f32[129,512]{1,0:T(8,128)S(1)}, f32[129,512]{1,0:T(8,128)S(1)})) conditional(s32[]{:T(128)} %convert_element_type.331, (f32[129,512]{1,0:T(8,128)S(1)}, f32[129,512]{1,0:T(8,128)S(1)}) %tuple.76, (pred[]{:T(512)}, s32[]{:T(128)}, pred[]{:T(512)}, bf16[4096,512]{1,0:T(8,128)(2,1)}, bf16[129,128]{1,0:T(8,128)(2,1)S(1)}, ...), branch_computations={%region_3.3_spmd, %region_4.6_spmd} | conditional | flops 136190976 | bytes 6068488 | solution.py:123
  325.2 4.5 conditional
  330.0 8.9 %conditional.5 = ((f32[129,512]{1,0:T(8,128)S(1)}, f32[129,512]{1,0:T(8,128)S(1)})) conditional(s32[]{:T(128)} %convert_element_type.331, (f32[129,512]{1,0:T(8,128)S(1)}, f32[129,512]{1,0:T(8,128)S(1)}) %tuple.76, (pred[]{:T(512)}, s32[]{:T(128)}, pred[]{:T(512)}, bf16[4096,512]{1,0:T(8,128)(2,1)}, bf16[129,128]{1,0:T(8,128)(2,1)S(1)}, ...), branch_computations={%region_3.3_spmd, %region_4.6_spmd} | conditional | flops 136190976 | bytes 6068488 | solution.py:123
  334.4 4.5 conditional
  339.2 8.9 %conditional.5 = ((f32[129,512]{1,0:T(8,128)S(1)}, f32[129,512]{1,0:T(8,128)S(1)})) conditional(s32[]{:T(128)} %convert_element_type.331, (f32[129,512]{1,0:T(8,128)S(1)}, f32[129,512]{1,0:T(8,128)S(1)}) %tuple.76, (pred[]{:T(512)}, s32[]{:T(128)}, pred[]{:T(512)}, bf16[4096,512]{1,0:T(8,128)(2,1)}, bf16[129,128]{1,0:T(8,128)(2,1)S(1)}, ...), branch_computations={%region_3.3_spmd, %region_4.6_spmd} | conditional | flops 136190976 | bytes 6068488 | solution.py:123
  343.6 4.5 conditional
  348.4 8.9 %conditional.5 = ((f32[129,512]{1,0:T(8,128)S(1)}, f32[129,512]{1,0:T(8,128)S(1)})) conditional(s32[]{:T(128)} %convert_element_type.331, (f32[129,512]{1,0:T(8,128)S(1)}, f32[129,512]{1,0:T(8,128)S(1)}) %tuple.76, (pred[]{:T(512)}, s32[]{:T(128)}, pred[]{:T(512)}, bf16[4096,512]{1,0:T(8,128)(2,1)}, bf16[129,128]{1,0:T(8,128)(2,1)S(1)}, ...), branch_computations={%region_3.3_spmd, %region_4.6_spmd} | conditional | flops 136190976 | bytes 6068488 | solution.py:123
  352.8 4.5 conditional
  357.7 8.9 %conditional.5 = ((f32[129,512]{1,0:T(8,128)S(1)}, f32[129,512]{1,0:T(8,128)S(1)})) conditional(s32[]{:T(128)} %convert_element_type.331, (f32[129,512]{1,0:T(8,128)S(1)}, f32[129,512]{1,0:T(8,128)S(1)}) %tuple.76, (pred[]{:T(512)}, s32[]{:T(128)}, pred[]{:T(512)}, bf16[4096,512]{1,0:T(8,128)(2,1)}, bf16[129,128]{1,0:T(8,128)(2,1)S(1)}, ...), branch_computations={%region_3.3_spmd, %region_4.6_spmd} | conditional | flops 136190976 | bytes 6068488 | solution.py:123
  362.0 4.5 conditional
  366.9 8.9 %conditional.5 = ((f32[129,512]{1,0:T(8,128)S(1)}, f32[129,512]{1,0:T(8,128)S(1)})) conditional(s32[]{:T(128)} %convert_element_type.331, (f32[129,512]{1,0:T(8,128)S(1)}, f32[129,512]{1,0:T(8,128)S(1)}) %tuple.76, (pred[]{:T(512)}, s32[]{:T(128)}, pred[]{:T(512)}, bf16[4096,512]{1,0:T(8,128)(2,1)}, bf16[129,128]{1,0:T(8,128)(2,1)S(1)}, ...), branch_computations={%region_3.3_spmd, %region_4.6_spmd} | conditional | flops 136190976 | bytes 6068488 | solution.py:123
  371.2 4.5 conditional
  376.1 8.9 %conditional.5 = ((f32[129,512]{1,0:T(8,128)S(1)}, f32[129,512]{1,0:T(8,128)S(1)})) conditional(s32[]{:T(128)} %convert_element_type.331, (f32[129,512]{1,0:T(8,128)S(1)}, f32[129,512]{1,0:T(8,128)S(1)}) %tuple.76, (pred[]{:T(512)}, s32[]{:T(128)}, pred[]{:T(512)}, bf16[4096,512]{1,0:T(8,128)(2,1)}, bf16[129,128]{1,0:T(8,128)(2,1)S(1)}, ...), branch_computations={%region_3.3_spmd, %region_4.6_spmd} | conditional | flops 136190976 | bytes 6068488 | solution.py:123
  380.5 4.5 conditional
  385.3 8.9 %conditional.5 = ((f32[129,512]{1,0:T(8,128)S(1)}, f32[129,512]{1,0:T(8,128)S(1)})) conditional(s32[]{:T(128)} %convert_element_type.331, (f32[129,512]{1,0:T(8,128)S(1)}, f32[129,512]{1,0:T(8,128)S(1)}) %tuple.76, (pred[]{:T(512)}, s32[]{:T(128)}, pred[]{:T(512)}, bf16[4096,512]{1,0:T(8,128)(2,1)}, bf16[129,128]{1,0:T(8,128)(2,1)S(1)}, ...), branch_computations={%region_3.3_spmd, %region_4.6_spmd} | conditional | flops 136190976 | bytes 6068488 | solution.py:123
  394.5 8.9 %conditional.5 = ((f32[129,512]{1,0:T(8,128)S(1)}, f32[129,512]{1,0:T(8,128)S(1)})) conditional(s32[]{:T(128)} %convert_element_type.331, (f32[129,512]{1,0:T(8,128)S(1)}, f32[129,512]{1,0:T(8,128)S(1)}) %tuple.76, (pred[]{:T(512)}, s32[]{:T(128)}, pred[]{:T(512)}, bf16[4096,512]{1,0:T(8,128)(2,1)}, bf16[129,128]{1,0:T(8,128)(2,1)S(1)}, ...), branch_computations={%region_3.3_spmd, %region_4.6_spmd} | conditional | flops 136190976 | bytes 6068488 | solution.py:123
  398.9 4.5 conditional
  403.7 8.9 %conditional.5 = ((f32[129,512]{1,0:T(8,128)S(1)}, f32[129,512]{1,0:T(8,128)S(1)})) conditional(s32[]{:T(128)} %convert_element_type.331, (f32[129,512]{1,0:T(8,128)S(1)}, f32[129,512]{1,0:T(8,128)S(1)}) %tuple.76, (pred[]{:T(512)}, s32[]{:T(128)}, pred[]{:T(512)}, bf16[4096,512]{1,0:T(8,128)(2,1)}, bf16[129,128]{1,0:T(8,128)(2,1)S(1)}, ...), branch_computations={%region_3.3_spmd, %region_4.6_spmd} | conditional | flops 136190976 | bytes 6068488 | solution.py:123
  412.9 8.9 %conditional.5 = ((f32[129,512]{1,0:T(8,128)S(1)}, f32[129,512]{1,0:T(8,128)S(1)})) conditional(s32[]{:T(128)} %convert_element_type.331, (f32[129,512]{1,0:T(8,128)S(1)}, f32[129,512]{1,0:T(8,128)S(1)}) %tuple.76, (pred[]{:T(512)}, s32[]{:T(128)}, pred[]{:T(512)}, bf16[4096,512]{1,0:T(8,128)(2,1)}, bf16[129,128]{1,0:T(8,128)(2,1)S(1)}, ...), branch_computations={%region_3.3_spmd, %region_4.6_spmd} | conditional | flops 136190976 | bytes 6068488 | solution.py:123
  417.3 4.5 conditional
  422.1 8.9 %conditional.5 = ((f32[129,512]{1,0:T(8,128)S(1)}, f32[129,512]{1,0:T(8,128)S(1)})) conditional(s32[]{:T(128)} %convert_element_type.331, (f32[129,512]{1,0:T(8,128)S(1)}, f32[129,512]{1,0:T(8,128)S(1)}) %tuple.76, (pred[]{:T(512)}, s32[]{:T(128)}, pred[]{:T(512)}, bf16[4096,512]{1,0:T(8,128)(2,1)}, bf16[129,128]{1,0:T(8,128)(2,1)S(1)}, ...), branch_computations={%region_3.3_spmd, %region_4.6_spmd} | conditional | flops 136190976 | bytes 6068488 | solution.py:123
  431.4 8.9 %conditional.5 = ((f32[129,512]{1,0:T(8,128)S(1)}, f32[129,512]{1,0:T(8,128)S(1)})) conditional(s32[]{:T(128)} %convert_element_type.331, (f32[129,512]{1,0:T(8,128)S(1)}, f32[129,512]{1,0:T(8,128)S(1)}) %tuple.76, (pred[]{:T(512)}, s32[]{:T(128)}, pred[]{:T(512)}, bf16[4096,512]{1,0:T(8,128)(2,1)}, bf16[129,128]{1,0:T(8,128)(2,1)S(1)}, ...), branch_computations={%region_3.3_spmd, %region_4.6_spmd} | conditional | flops 136190976 | bytes 6068488 | solution.py:123
  440.6 8.9 %conditional.5 = ((f32[129,512]{1,0:T(8,128)S(1)}, f32[129,512]{1,0:T(8,128)S(1)})) conditional(s32[]{:T(128)} %convert_element_type.331, (f32[129,512]{1,0:T(8,128)S(1)}, f32[129,512]{1,0:T(8,128)S(1)}) %tuple.76, (pred[]{:T(512)}, s32[]{:T(128)}, pred[]{:T(512)}, bf16[4096,512]{1,0:T(8,128)(2,1)}, bf16[129,128]{1,0:T(8,128)(2,1)S(1)}, ...), branch_computations={%region_3.3_spmd, %region_4.6_spmd} | conditional | flops 136190976 | bytes 6068488 | solution.py:123
  445.0 4.5 conditional
  (329 shorter events, 318.0 us)
Async XLA Ops:
  6.5 75.1 %all-gather.5.cloned.1.call-start = ((), (), s32[]{:S(2)}) async-start(), calls=%async_computation.1 | async-start | bytes 4325376 | tf_op jit(solution)/shard_map/all_gather | solution.py:77
  7.3 147.3 %all-gather.3.cloned.1.call-start = ((), (), s32[]{:S(2)}) async-start(), calls=%async_computation | async-start | bytes 4325376 | tf_op jit(solution)/shard_map/all_gather | solution.py:94
  449.6 4.8 %copy-start = (bf16[128,512]{1,0:T(8,128)(2,1)S(1)}, bf16[128,512]{1,0:T(8,128)(2,1)}, u32[]{:S(2)}) copy-start(bf16[128,512]{1,0:T(8,128)(2,1)} %fusion.35) | copy-start | bytes 393220
  449.7 4.8 %copy-start.1 = (bf16[128,512]{1,0:T(8,128)(2,1)S(1)}, bf16[128,512]{1,0:T(8,128)(2,1)}, u32[]{:S(2)}) copy-start(bf16[128,512]{1,0:T(8,128)(2,1)} %param.15) | copy-start | bytes 393220
  449.7 4.8 %copy-start.2 = (f32[512]{0:T(512)S(1)}, f32[512]{0:T(512)}, u32[]{:S(2)}) copy-start(f32[512]{0:T(512)} %param.13) | copy-start | bytes 6148
  451.2 3.2 collective-permute-start
Sparse Core Ops, SparseCore 0:
  9.5 72.1 all-gather.4
  83.8 70.7 all-gather.2
where the time goes:
time: 467 us; the launch traced here: 462 us
  matrix products  282 us (60%)
  waiting for transfers between devices  117 us (25%)
  blocking collectives  28.1 us (6%)
  other arithmetic  14.2 us (3%)
  between operations  13.6 us (3%)
  loops' own time  5.88 us (1%)
    dot_general x128, matrix products, table_dot(): jnp.dot(table_pair[1], data, preferred_element_type=jnp.float32)  141 us
    dot_general x128, matrix products, table_dot(): jnp.dot(table_pair[0], data, preferred_element_type=jnp.float32)  138 us
    all_gather x1, waiting for transfers between devices, local(): segment_in = lax.all_gather(normed, 'ctx', axis=0, tiled=True)  72.9 us
    all_gather x1, waiting for transfers between devices, local(): whole_filter = lax.all_gather(filter_taps, 'ctx', axis=0, tiled=True)  41.6 us
    psum x1, blocking collectives, local(): row_power = lax.psum(jnp.sum(values * values, axis=1), 'ch') / C  28.1 us
    convert_element_type x36, other arithmetic, split_parts(): high = matrix.astype(jnp.bfloat16)  10.1 us
  transfers between devices with their start and end apart: 3, of which 3 were waited for; matrix products, arithmetic and copies ran while one was open for 1% of the time, Pallas kernels for 0%

commit v1 on v0

--- a/solution.py
+++ b/solution.py
@@ -62,7 +62,7 @@
     ctx_count = lax.axis_size("ctx")
     ctx_index = lax.axis_index("ctx")
     values = signal.astype(jnp.float32)
-    row_power = lax.psum(jnp.sum(values * values, axis=1), "ch") / C
+    row_power = jnp.sum(lax.all_gather(jnp.sum(values * values, axis=1), "ch"), 0) / C
     normed = (values * lax.rsqrt(row_power + EPS)[:, None] * norm_gain[None, :]).astype(
         jnp.bfloat16
     )

time: 467 us -> 467 us (level)
  blocking collectives: 28.1 us -> 16 us
  waiting for transfers between devices: 117 us -> 129 us
    psum x1 -> x0, blocking collectives: 28.1 us -> none  [local(): row_power = lax.psum(jnp.sum(values * values, axis=1), 'ch') / C]
    all_gather x0 -> x1, blocking collectives: none -> 16 us  [local(): lax.all_gather(jnp.sum(values * values, axis=1), 'ch')]
    all_gather x1, waiting for transfers between devices: 41.6 us -> 53.4 us  [local(): whole_filter = lax.all_gather(filter_taps, 'ctx', axis=0, tiled=True)]
where the time goes in v1:
time: 467 us; the launch traced here: 462 us
  matrix products  282 us (60%)
  waiting for transfers between devices  129 us (28%)
  blocking collectives  16 us (3%)
  other arithmetic  14.2 us (3%)
  between operations  13.6 us (3%)
  loops' own time  5.88 us (1%)
    dot_general x128, matrix products, table_dot(): jnp.dot(table_pair[1], data, preferred_element_type=jnp.float32)  141 us
    dot_general x128, matrix products, table_dot(): jnp.dot(table_pair[0], data, preferred_element_type=jnp.float32)  138 us
    all_gather x1, waiting for transfers between devices, local(): segment_in = lax.all_gather(normed, 'ctx', axis=0, tiled=True)  73.1 us
    all_gather x1, waiting for transfers between devices, local(): whole_filter = lax.all_gather(filter_taps, 'ctx', axis=0, tiled=True)  53.4 us
    all_gather x1, blocking collectives, local(): lax.all_gather(jnp.sum(values * values, axis=1), 'ch')  16 us
    convert_element_type x36, other arithmetic, split_parts(): high = matrix.astype(jnp.bfloat16)  10.1 us
  transfers between devices with their start and end apart: 3, of which 3 were waited for; matrix products, arithmetic and copies ran while one was open for 1% of the time, Pallas kernels for 0%

profile of v1, /device:TPU:483, one launch (start us, length us, event | category | flops | bytes accessed | tf_op | source)
XLA Modules:
  0.0 462.2 jit_solution(11746377127055512951)
XLA Ops:
  8.3 16.0 %all-gather.1 = f32[16,1,128]{2,1,0:T(1,128)S(1)} all-gather(f32[1,1,128]{2,1,0:T(1,128)S(1)} %bitcast.37), channel_id=2, replica_groups=mesh['ctx'=32,'ch'=16] {'ch'}, dimensions={0}, use_global_device_ids=true | all-gather | bytes 8704 | tf_op jit(solution)/shard_map/all_gather | solution.py:65
  28.1 53.4 %all-gather.7.cloned.1.call-done = bf16[4096,512]{1,0:T(8,128)(2,1)} async-done(((bf16[128,512]{1,0:T(8,128)(2,1)}), bf16[4096,512]{1,0:T(8,128)(2,1)}) %all-gather.7.cloned.1.call-update) | async-done | bytes 4194320 | tf_op jit(solution)/shard_map/all_gather | solution.py:77
  81.5 73.1 %all-gather.5.cloned.1.call-done = bf16[4096,512]{1,0:T(8,128)(2,1)} async-done(((bf16[128,512]{1,0:T(8,128)(2,1)}), bf16[4096,512]{1,0:T(8,128)(2,1)}) %all-gather.5.cloned.1.call-update) | async-done | bytes 4194320 | tf_op jit(solution)/shard_map/all_gather | solution.py:94
  154.6 294.8 %while.19 = (s32[]{:T(128)}, f32[129,512]{1,0:T(8,128)S(1)}, f32[129,512]{1,0:T(8,128)S(1)}, s32[]{:T(128)}, bf16[4096,512]{1,0:T(8,128)(2,1)}, /*index=5*/bf16[...) while((s32[]{:T(128)}, f32[129,512]{1,0:T(8,128)S(1)}, ...), condition=%wide.region_7.8_spmd.clone.clone, body=%wide.region_2.7_spmd.clone.clone.sunk | while | flops 136455184 | bytes 6134993 | solution.py:125
  155.0 8.9 %conditional.5 = ((f32[129,512]{1,0:T(8,128)S(1)}, f32[129,512]{1,0:T(8,128)S(1)})) conditional(s32[]{:T(128)} %convert_element_type.331, (f32[129,512]{1,0:T(8,128)S(1)}, f32[129,512]{1,0:T(8,128)S(1)}) %tuple.76, (pred[]{:T(512)}, s32[]{:T(128)}, pred[]{:T(512)}, bf16[4096,512]{1,0:T(8,128)(2,1)}, bf16[129,128]{1,0:T(8,128)(2,1)S(1)}, ...), branch_computations={%region_3.3_spmd, %region_4.6_spmd} | conditional | flops 136190976 | bytes 6068488 | solution.py:123
  159.4 4.5 conditional
  164.2 8.9 %conditional.5 = ((f32[129,512]{1,0:T(8,128)S(1)}, f32[129,512]{1,0:T(8,128)S(1)})) conditional(s32[]{:T(128)} %convert_element_type.331, (f32[129,512]{1,0:T(8,128)S(1)}, f32[129,512]{1,0:T(8,128)S(1)}) %tuple.76, (pred[]{:T(512)}, s32[]{:T(128)}, pred[]{:T(512)}, bf16[4096,512]{1,0:T(8,128)(2,1)}, bf16[129,128]{1,0:T(8,128)(2,1)S(1)}, ...), branch_computations={%region_3.3_spmd, %region_4.6_spmd} | conditional | flops 136190976 | bytes 6068488 | solution.py:123
  168.6 4.5 conditional
  173.4 8.9 %conditional.5 = ((f32[129,512]{1,0:T(8,128)S(1)}, f32[129,512]{1,0:T(8,128)S(1)})) conditional(s32[]{:T(128)} %convert_element_type.331, (f32[129,512]{1,0:T(8,128)S(1)}, f32[129,512]{1,0:T(8,128)S(1)}) %tuple.76, (pred[]{:T(512)}, s32[]{:T(128)}, pred[]{:T(512)}, bf16[4096,512]{1,0:T(8,128)(2,1)}, bf16[129,128]{1,0:T(8,128)(2,1)S(1)}, ...), branch_computations={%region_3.3_spmd, %region_4.6_spmd} | conditional | flops 136190976 | bytes 6068488 | solution.py:123
  177.8 4.5 conditional
  182.6 8.9 %conditional.5 = ((f32[129,512]{1,0:T(8,128)S(1)}, f32[129,512]{1,0:T(8,128)S(1)})) conditional(s32[]{:T(128)} %convert_element_type.331, (f32[129,512]{1,0:T(8,128)S(1)}, f32[129,512]{1,0:T(8,128)S(1)}) %tuple.76, (pred[]{:T(512)}, s32[]{:T(128)}, pred[]{:T(512)}, bf16[4096,512]{1,0:T(8,128)(2,1)}, bf16[129,128]{1,0:T(8,128)(2,1)S(1)}, ...), branch_computations={%region_3.3_spmd, %region_4.6_spmd} | conditional | flops 136190976 | bytes 6068488 | solution.py:123
  187.0 4.5 conditional
  191.8 8.9 %conditional.5 = ((f32[129,512]{1,0:T(8,128)S(1)}, f32[129,512]{1,0:T(8,128)S(1)})) conditional(s32[]{:T(128)} %convert_element_type.331, (f32[129,512]{1,0:T(8,128)S(1)}, f32[129,512]{1,0:T(8,128)S(1)}) %tuple.76, (pred[]{:T(512)}, s32[]{:T(128)}, pred[]{:T(512)}, bf16[4096,512]{1,0:T(8,128)(2,1)}, bf16[129,128]{1,0:T(8,128)(2,1)S(1)}, ...), branch_computations={%region_3.3_spmd, %region_4.6_spmd} | conditional | flops 136190976 | bytes 6068488 | solution.py:123
  196.2 4.5 conditional
  201.0 8.9 %conditional.5 = ((f32[129,512]{1,0:T(8,128)S(1)}, f32[129,512]{1,0:T(8,128)S(1)})) conditional(s32[]{:T(128)} %convert_element_type.331, (f32[129,512]{1,0:T(8,128)S(1)}, f32[129,512]{1,0:T(8,128)S(1)}) %tuple.76, (pred[]{:T(512)}, s32[]{:T(128)}, pred[]{:T(512)}, bf16[4096,512]{1,0:T(8,128)(2,1)}, bf16[129,128]{1,0:T(8,128)(2,1)S(1)}, ...), branch_computations={%region_3.3_spmd, %region_4.6_spmd} | conditional | flops 136190976 | bytes 6068488 | solution.py:123
  205.4 4.5 conditional
  210.3 8.9 %conditional.5 = ((f32[129,512]{1,0:T(8,128)S(1)}, f32[129,512]{1,0:T(8,128)S(1)})) conditional(s32[]{:T(128)} %convert_element_type.331, (f32[129,512]{1,0:T(8,128)S(1)}, f32[129,512]{1,0:T(8,128)S(1)}) %tuple.76, (pred[]{:T(512)}, s32[]{:T(128)}, pred[]{:T(512)}, bf16[4096,512]{1,0:T(8,128)(2,1)}, bf16[129,128]{1,0:T(8,128)(2,1)S(1)}, ...), branch_computations={%region_3.3_spmd, %region_4.6_spmd} | conditional | flops 136190976 | bytes 6068488 | solution.py:123
  214.6 4.5 conditional
  219.5 8.9 %conditional.5 = ((f32[129,512]{1,0:T(8,128)S(1)}, f32[129,512]{1,0:T(8,128)S(1)})) conditional(s32[]{:T(128)} %convert_element_type.331, (f32[129,512]{1,0:T(8,128)S(1)}, f32[129,512]{1,0:T(8,128)S(1)}) %tuple.76, (pred[]{:T(512)}, s32[]{:T(128)}, pred[]{:T(512)}, bf16[4096,512]{1,0:T(8,128)(2,1)}, bf16[129,128]{1,0:T(8,128)(2,1)S(1)}, ...), branch_computations={%region_3.3_spmd, %region_4.6_spmd} | conditional | flops 136190976 | bytes 6068488 | solution.py:123
  223.8 4.5 conditional
  228.7 8.9 %conditional.5 = ((f32[129,512]{1,0:T(8,128)S(1)}, f32[129,512]{1,0:T(8,128)S(1)})) conditional(s32[]{:T(128)} %convert_element_type.331, (f32[129,512]{1,0:T(8,128)S(1)}, f32[129,512]{1,0:T(8,128)S(1)}) %tuple.76, (pred[]{:T(512)}, s32[]{:T(128)}, pred[]{:T(512)}, bf16[4096,512]{1,0:T(8,128)(2,1)}, bf16[129,128]{1,0:T(8,128)(2,1)S(1)}, ...), branch_computations={%region_3.3_spmd, %region_4.6_spmd} | conditional | flops 136190976 | bytes 6068488 | solution.py:123
  233.1 4.5 conditional
  237.9 8.9 %conditional.5 = ((f32[129,512]{1,0:T(8,128)S(1)}, f32[129,512]{1,0:T(8,128)S(1)})) conditional(s32[]{:T(128)} %convert_element_type.331, (f32[129,512]{1,0:T(8,128)S(1)}, f32[129,512]{1,0:T(8,128)S(1)}) %tuple.76, (pred[]{:T(512)}, s32[]{:T(128)}, pred[]{:T(512)}, bf16[4096,512]{1,0:T(8,128)(2,1)}, bf16[129,128]{1,0:T(8,128)(2,1)S(1)}, ...), branch_computations={%region_3.3_spmd, %region_4.6_spmd} | conditional | flops 136190976 | bytes 6068488 | solution.py:123
  242.3 4.5 conditional
  247.1 8.9 %conditional.5 = ((f32[129,512]{1,0:T(8,128)S(1)}, f32[129,512]{1,0:T(8,128)S(1)})) conditional(s32[]{:T(128)} %convert_element_type.331, (f32[129,512]{1,0:T(8,128)S(1)}, f32[129,512]{1,0:T(8,128)S(1)}) %tuple.76, (pred[]{:T(512)}, s32[]{:T(128)}, pred[]{:T(512)}, bf16[4096,512]{1,0:T(8,128)(2,1)}, bf16[129,128]{1,0:T(8,128)(2,1)S(1)}, ...), branch_computations={%region_3.3_spmd, %region_4.6_spmd} | conditional | flops 136190976 | bytes 6068488 | solution.py:123
  251.5 4.5 conditional
  256.3 8.9 %conditional.5 = ((f32[129,512]{1,0:T(8,128)S(1)}, f32[129,512]{1,0:T(8,128)S(1)})) conditional(s32[]{:T(128)} %convert_element_type.331, (f32[129,512]{1,0:T(8,128)S(1)}, f32[129,512]{1,0:T(8,128)S(1)}) %tuple.76, (pred[]{:T(512)}, s32[]{:T(128)}, pred[]{:T(512)}, bf16[4096,512]{1,0:T(8,128)(2,1)}, bf16[129,128]{1,0:T(8,128)(2,1)S(1)}, ...), branch_computations={%region_3.3_spmd, %region_4.6_spmd} | conditional | flops 136190976 | bytes 6068488 | solution.py:123
  260.7 4.5 conditional
  265.5 8.9 %conditional.5 = ((f32[129,512]{1,0:T(8,128)S(1)}, f32[129,512]{1,0:T(8,128)S(1)})) conditional(s32[]{:T(128)} %convert_element_type.331, (f32[129,512]{1,0:T(8,128)S(1)}, f32[129,512]{1,0:T(8,128)S(1)}) %tuple.76, (pred[]{:T(512)}, s32[]{:T(128)}, pred[]{:T(512)}, bf16[4096,512]{1,0:T(8,128)(2,1)}, bf16[129,128]{1,0:T(8,128)(2,1)S(1)}, ...), branch_computations={%region_3.3_spmd, %region_4.6_spmd} | conditional | flops 136190976 | bytes 6068488 | solution.py:123
  269.9 4.5 conditional
  274.7 8.9 %conditional.5 = ((f32[129,512]{1,0:T(8,128)S(1)}, f32[129,512]{1,0:T(8,128)S(1)})) conditional(s32[]{:T(128)} %convert_element_type.331, (f32[129,512]{1,0:T(8,128)S(1)}, f32[129,512]{1,0:T(8,128)S(1)}) %tuple.76, (pred[]{:T(512)}, s32[]{:T(128)}, pred[]{:T(512)}, bf16[4096,512]{1,0:T(8,128)(2,1)}, bf16[129,128]{1,0:T(8,128)(2,1)S(1)}, ...), branch_computations={%region_3.3_spmd, %region_4.6_spmd} | conditional | flops 136190976 | bytes 6068488 | solution.py:123
  279.1 4.5 conditional
  284.0 8.9 %conditional.5 = ((f32[129,512]{1,0:T(8,128)S(1)}, f32[129,512]{1,0:T(8,128)S(1)})) conditional(s32[]{:T(128)} %convert_element_type.331, (f32[129,512]{1,0:T(8,128)S(1)}, f32[129,512]{1,0:T(8,128)S(1)}) %tuple.76, (pred[]{:T(512)}, s32[]{:T(128)}, pred[]{:T(512)}, bf16[4096,512]{1,0:T(8,128)(2,1)}, bf16[129,128]{1,0:T(8,128)(2,1)S(1)}, ...), branch_computations={%region_3.3_spmd, %region_4.6_spmd} | conditional | flops 136190976 | bytes 6068488 | solution.py:123
  288.3 4.5 conditional
  293.2 8.9 %conditional.5 = ((f32[129,512]{1,0:T(8,128)S(1)}, f32[129,512]{1,0:T(8,128)S(1)})) conditional(s32[]{:T(128)} %convert_element_type.331, (f32[129,512]{1,0:T(8,128)S(1)}, f32[129,512]{1,0:T(8,128)S(1)}) %tuple.76, (pred[]{:T(512)}, s32[]{:T(128)}, pred[]{:T(512)}, bf16[4096,512]{1,0:T(8,128)(2,1)}, bf16[129,128]{1,0:T(8,128)(2,1)S(1)}, ...), branch_computations={%region_3.3_spmd, %region_4.6_spmd} | conditional | flops 136190976 | bytes 6068488 | solution.py:123
  297.5 4.5 conditional
  302.4 8.9 %conditional.5 = ((f32[129,512]{1,0:T(8,128)S(1)}, f32[129,512]{1,0:T(8,128)S(1)})) conditional(s32[]{:T(128)} %convert_element_type.331, (f32[129,512]{1,0:T(8,128)S(1)}, f32[129,512]{1,0:T(8,128)S(1)}) %tuple.76, (pred[]{:T(512)}, s32[]{:T(128)}, pred[]{:T(512)}, bf16[4096,512]{1,0:T(8,128)(2,1)}, bf16[129,128]{1,0:T(8,128)(2,1)S(1)}, ...), branch_computations={%region_3.3_spmd, %region_4.6_spmd} | conditional | flops 136190976 | bytes 6068488 | solution.py:123
  306.8 4.5 conditional
  311.6 8.9 %conditional.5 = ((f32[129,512]{1,0:T(8,128)S(1)}, f32[129,512]{1,0:T(8,128)S(1)})) conditional(s32[]{:T(128)} %convert_element_type.331, (f32[129,512]{1,0:T(8,128)S(1)}, f32[129,512]{1,0:T(8,128)S(1)}) %tuple.76, (pred[]{:T(512)}, s32[]{:T(128)}, pred[]{:T(512)}, bf16[4096,512]{1,0:T(8,128)(2,1)}, bf16[129,128]{1,0:T(8,128)(2,1)S(1)}, ...), branch_computations={%region_3.3_spmd, %region_4.6_spmd} | conditional | flops 136190976 | bytes 6068488 | solution.py:123
  316.0 4.5 conditional
  320.8 8.9 %conditional.5 = ((f32[129,512]{1,0:T(8,128)S(1)}, f32[129,512]{1,0:T(8,128)S(1)})) conditional(s32[]{:T(128)} %convert_element_type.331, (f32[129,512]{1,0:T(8,128)S(1)}, f32[129,512]{1,0:T(8,128)S(1)}) %tuple.76, (pred[]{:T(512)}, s32[]{:T(128)}, pred[]{:T(512)}, bf16[4096,512]{1,0:T(8,128)(2,1)}, bf16[129,128]{1,0:T(8,128)(2,1)S(1)}, ...), branch_computations={%region_3.3_spmd, %region_4.6_spmd} | conditional | flops 136190976 | bytes 6068488 | solution.py:123
  325.2 4.5 conditional
  330.0 8.9 %conditional.5 = ((f32[129,512]{1,0:T(8,128)S(1)}, f32[129,512]{1,0:T(8,128)S(1)})) conditional(s32[]{:T(128)} %convert_element_type.331, (f32[129,512]{1,0:T(8,128)S(1)}, f32[129,512]{1,0:T(8,128)S(1)}) %tuple.76, (pred[]{:T(512)}, s32[]{:T(128)}, pred[]{:T(512)}, bf16[4096,512]{1,0:T(8,128)(2,1)}, bf16[129,128]{1,0:T(8,128)(2,1)S(1)}, ...), branch_computations={%region_3.3_spmd, %region_4.6_spmd} | conditional | flops 136190976 | bytes 6068488 | solution.py:123
  334.4 4.5 conditional
  339.2 8.9 %conditional.5 = ((f32[129,512]{1,0:T(8,128)S(1)}, f32[129,512]{1,0:T(8,128)S(1)})) conditional(s32[]{:T(128)} %convert_element_type.331, (f32[129,512]{1,0:T(8,128)S(1)}, f32[129,512]{1,0:T(8,128)S(1)}) %tuple.76, (pred[]{:T(512)}, s32[]{:T(128)}, pred[]{:T(512)}, bf16[4096,512]{1,0:T(8,128)(2,1)}, bf16[129,128]{1,0:T(8,128)(2,1)S(1)}, ...), branch_computations={%region_3.3_spmd, %region_4.6_spmd} | conditional | flops 136190976 | bytes 6068488 | solution.py:123
  343.6 4.5 conditional
  348.4 8.9 %conditional.5 = ((f32[129,512]{1,0:T(8,128)S(1)}, f32[129,512]{1,0:T(8,128)S(1)})) conditional(s32[]{:T(128)} %convert_element_type.331, (f32[129,512]{1,0:T(8,128)S(1)}, f32[129,512]{1,0:T(8,128)S(1)}) %tuple.76, (pred[]{:T(512)}, s32[]{:T(128)}, pred[]{:T(512)}, bf16[4096,512]{1,0:T(8,128)(2,1)}, bf16[129,128]{1,0:T(8,128)(2,1)S(1)}, ...), branch_computations={%region_3.3_spmd, %region_4.6_spmd} | conditional | flops 136190976 | bytes 6068488 | solution.py:123
  352.8 4.5 conditional
  357.7 8.9 %conditional.5 = ((f32[129,512]{1,0:T(8,128)S(1)}, f32[129,512]{1,0:T(8,128)S(1)})) conditional(s32[]{:T(128)} %convert_element_type.331, (f32[129,512]{1,0:T(8,128)S(1)}, f32[129,512]{1,0:T(8,128)S(1)}) %tuple.76, (pred[]{:T(512)}, s32[]{:T(128)}, pred[]{:T(512)}, bf16[4096,512]{1,0:T(8,128)(2,1)}, bf16[129,128]{1,0:T(8,128)(2,1)S(1)}, ...), branch_computations={%region_3.3_spmd, %region_4.6_spmd} | conditional | flops 136190976 | bytes 6068488 | solution.py:123
  362.0 4.5 conditional
  366.9 8.9 %conditional.5 = ((f32[129,512]{1,0:T(8,128)S(1)}, f32[129,512]{1,0:T(8,128)S(1)})) conditional(s32[]{:T(128)} %convert_element_type.331, (f32[129,512]{1,0:T(8,128)S(1)}, f32[129,512]{1,0:T(8,128)S(1)}) %tuple.76, (pred[]{:T(512)}, s32[]{:T(128)}, pred[]{:T(512)}, bf16[4096,512]{1,0:T(8,128)(2,1)}, bf16[129,128]{1,0:T(8,128)(2,1)S(1)}, ...), branch_computations={%region_3.3_spmd, %region_4.6_spmd} | conditional | flops 136190976 | bytes 6068488 | solution.py:123
  371.2 4.5 conditional
  376.1 8.9 %conditional.5 = ((f32[129,512]{1,0:T(8,128)S(1)}, f32[129,512]{1,0:T(8,128)S(1)})) conditional(s32[]{:T(128)} %convert_element_type.331, (f32[129,512]{1,0:T(8,128)S(1)}, f32[129,512]{1,0:T(8,128)S(1)}) %tuple.76, (pred[]{:T(512)}, s32[]{:T(128)}, pred[]{:T(512)}, bf16[4096,512]{1,0:T(8,128)(2,1)}, bf16[129,128]{1,0:T(8,128)(2,1)S(1)}, ...), branch_computations={%region_3.3_spmd, %region_4.6_spmd} | conditional | flops 136190976 | bytes 6068488 | solution.py:123
  380.5 4.5 conditional
  385.3 8.9 %conditional.5 = ((f32[129,512]{1,0:T(8,128)S(1)}, f32[129,512]{1,0:T(8,128)S(1)})) conditional(s32[]{:T(128)} %convert_element_type.331, (f32[129,512]{1,0:T(8,128)S(1)}, f32[129,512]{1,0:T(8,128)S(1)}) %tuple.76, (pred[]{:T(512)}, s32[]{:T(128)}, pred[]{:T(512)}, bf16[4096,512]{1,0:T(8,128)(2,1)}, bf16[129,128]{1,0:T(8,128)(2,1)S(1)}, ...), branch_computations={%region_3.3_spmd, %region_4.6_spmd} | conditional | flops 136190976 | bytes 6068488 | solution.py:123
  394.5 8.9 %conditional.5 = ((f32[129,512]{1,0:T(8,128)S(1)}, f32[129,512]{1,0:T(8,128)S(1)})) conditional(s32[]{:T(128)} %convert_element_type.331, (f32[129,512]{1,0:T(8,128)S(1)}, f32[129,512]{1,0:T(8,128)S(1)}) %tuple.76, (pred[]{:T(512)}, s32[]{:T(128)}, pred[]{:T(512)}, bf16[4096,512]{1,0:T(8,128)(2,1)}, bf16[129,128]{1,0:T(8,128)(2,1)S(1)}, ...), branch_computations={%region_3.3_spmd, %region_4.6_spmd} | conditional | flops 136190976 | bytes 6068488 | solution.py:123
  398.9 4.5 conditional
  403.7 8.9 %conditional.5 = ((f32[129,512]{1,0:T(8,128)S(1)}, f32[129,512]{1,0:T(8,128)S(1)})) conditional(s32[]{:T(128)} %convert_element_type.331, (f32[129,512]{1,0:T(8,128)S(1)}, f32[129,512]{1,0:T(8,128)S(1)}) %tuple.76, (pred[]{:T(512)}, s32[]{:T(128)}, pred[]{:T(512)}, bf16[4096,512]{1,0:T(8,128)(2,1)}, bf16[129,128]{1,0:T(8,128)(2,1)S(1)}, ...), branch_computations={%region_3.3_spmd, %region_4.6_spmd} | conditional | flops 136190976 | bytes 6068488 | solution.py:123
  412.9 8.9 %conditional.5 = ((f32[129,512]{1,0:T(8,128)S(1)}, f32[129,512]{1,0:T(8,128)S(1)})) conditional(s32[]{:T(128)} %convert_element_type.331, (f32[129,512]{1,0:T(8,128)S(1)}, f32[129,512]{1,0:T(8,128)S(1)}) %tuple.76, (pred[]{:T(512)}, s32[]{:T(128)}, pred[]{:T(512)}, bf16[4096,512]{1,0:T(8,128)(2,1)}, bf16[129,128]{1,0:T(8,128)(2,1)S(1)}, ...), branch_computations={%region_3.3_spmd, %region_4.6_spmd} | conditional | flops 136190976 | bytes 6068488 | solution.py:123
  417.3 4.5 conditional
  422.1 8.9 %conditional.5 = ((f32[129,512]{1,0:T(8,128)S(1)}, f32[129,512]{1,0:T(8,128)S(1)})) conditional(s32[]{:T(128)} %convert_element_type.331, (f32[129,512]{1,0:T(8,128)S(1)}, f32[129,512]{1,0:T(8,128)S(1)}) %tuple.76, (pred[]{:T(512)}, s32[]{:T(128)}, pred[]{:T(512)}, bf16[4096,512]{1,0:T(8,128)(2,1)}, bf16[129,128]{1,0:T(8,128)(2,1)S(1)}, ...), branch_computations={%region_3.3_spmd, %region_4.6_spmd} | conditional | flops 136190976 | bytes 6068488 | solution.py:123
  431.4 8.9 %conditional.5 = ((f32[129,512]{1,0:T(8,128)S(1)}, f32[129,512]{1,0:T(8,128)S(1)})) conditional(s32[]{:T(128)} %convert_element_type.331, (f32[129,512]{1,0:T(8,128)S(1)}, f32[129,512]{1,0:T(8,128)S(1)}) %tuple.76, (pred[]{:T(512)}, s32[]{:T(128)}, pred[]{:T(512)}, bf16[4096,512]{1,0:T(8,128)(2,1)}, bf16[129,128]{1,0:T(8,128)(2,1)S(1)}, ...), branch_computations={%region_3.3_spmd, %region_4.6_spmd} | conditional | flops 136190976 | bytes 6068488 | solution.py:123
  440.6 8.9 %conditional.5 = ((f32[129,512]{1,0:T(8,128)S(1)}, f32[129,512]{1,0:T(8,128)S(1)})) conditional(s32[]{:T(128)} %convert_element_type.331, (f32[129,512]{1,0:T(8,128)S(1)}, f32[129,512]{1,0:T(8,128)S(1)}) %tuple.76, (pred[]{:T(512)}, s32[]{:T(128)}, pred[]{:T(512)}, bf16[4096,512]{1,0:T(8,128)(2,1)}, bf16[129,128]{1,0:T(8,128)(2,1)S(1)}, ...), branch_computations={%region_3.3_spmd, %region_4.6_spmd} | conditional | flops 136190976 | bytes 6068488 | solution.py:123
  445.0 4.5 conditional
  (330 shorter events, 318.0 us)
Async XLA Ops:
  6.5 74.9 %all-gather.7.cloned.1.call-start = ((), (), s32[]{:S(2)}) async-start(), calls=%async_computation.1 | async-start | bytes 4325376 | tf_op jit(solution)/shard_map/all_gather | solution.py:77
  7.3 147.3 %all-gather.5.cloned.1.call-start = ((), (), s32[]{:S(2)}) async-start(), calls=%async_computation | async-start | bytes 4325376 | tf_op jit(solution)/shard_map/all_gather | solution.py:94
  449.6 4.8 %copy-start = (bf16[128,512]{1,0:T(8,128)(2,1)S(1)}, bf16[128,512]{1,0:T(8,128)(2,1)}, u32[]{:S(2)}) copy-start(bf16[128,512]{1,0:T(8,128)(2,1)} %fusion.35) | copy-start | bytes 393220
  449.7 4.8 %copy-start.1 = (bf16[128,512]{1,0:T(8,128)(2,1)S(1)}, bf16[128,512]{1,0:T(8,128)(2,1)}, u32[]{:S(2)}) copy-start(bf16[128,512]{1,0:T(8,128)(2,1)} %param.15) | copy-start | bytes 393220
  449.7 4.8 %copy-start.2 = (f32[512]{0:T(512)S(1)}, f32[512]{0:T(512)}, u32[]{:S(2)}) copy-start(f32[512]{0:T(512)} %param.13) | copy-start | bytes 6148
  451.2 3.2 collective-permute-start
Sparse Core Ops, SparseCore 0:
  9.5 71.9 all-gather.6
  83.6 70.9 all-gather.4
